TPU v7x, 32 devices: a whole 2x2x4 slice. The times are simulated.
32 devices in a mesh: groups: 2 (over y), tok: 4 (over z), mod: 2 (over x), fsdp: 2 (over core).
Axes of the slice: x: 2, y: 2, z: 4, core: 2. Of those that a mesh axis runs over, the one named last changes fastest.
Arguments:
- residual: bfloat16 [1024, 4096], P(('groups', 'tok'), ('fsdp', 'mod')), parts along dimension 0, may hold values from -30 to 30
- context: bfloat16 [1024, 4096], P(('groups', 'tok'), ('mod', 'fsdp')), parts along dimension 0, may hold values from -6 to 6
- out_proj: bfloat16 [4096, 4096], P('tok', ('fsdp', 'mod')), may hold values from -0.09375 to 0.09375
- norm_gain: bfloat16 [2, 4096], P(None, ('fsdp', 'mod')), may hold values from 0.099609375 to 1.8984375
- router_weight: bfloat16 [4096, 4], P(('fsdp', 'mod')), may hold values from -0.25 to 0.25
- block_modality: int32 [8], P(('groups', 'tok')), parts along dimension 0, may hold values from 0 to 1, as said below
- expert_rows: int32 [4, 128], P(None, ('groups', 'tok')), parts along dimension 1, may hold values from -1 to 127, as said below
- gate_weight: bfloat16 [4, 4096, 11008], P('mod', 'fsdp', 'tok'), may hold values from -0.09375 to 0.09375
- up_weight: bfloat16 [4, 4096, 11008], P('mod', 'fsdp', 'tok'), may hold values from -0.09375 to 0.09375
- down_weight: bfloat16 [4, 11008, 4096], P('mod', 'tok', 'fsdp'), may hold values from -0.0546875 to 0.0546875
Outputs:
- expert_out: bfloat16 [1024, 4096], P(('groups', 'tok'), ('fsdp', 'mod')), parts along dimension 0
There are 2 independent parts, one for each index of `groups`. A program takes and returns all parts, laid end to end along the dimension named above; an argument that names none is the same for every part. Nothing has to cross between parts.
Inputs may be any that keep to these rules, and one draw needn't show every extreme that they name: `block_modality`: both modalities occur in every window. `expert_rows`: slot s = t * 16 + j of expert e names a row among tokens t * 128 to (t + 1) * 128 - 1, or is -1 if unused. Experts below 2 take only text tokens, the others only image tokens; no expert takes a token twice; in each aligned block of 16 slots the used ones come first; every expert fills all 16 slots of at least one index of tok whose tokens have the expert's modality.
All inputs are finite; a program needn't handle non-finite values.
Results may differ from a plain program's by a relative error of at most 0.02.
Values may be sent and summed in bfloat16 or wider, within the bound.
No kernel may reach another device: no remote copies, remote signals or barrier semaphores. Data moves between devices by JAX's collectives and lax.ppermute only.
A program may use at most 192 MiB of HBM per device.

v0:
```python
import jax
import jax.numpy as jnp
from jax import lax
from jax.sharding import PartitionSpec as P

D = 4096
BLOCK = 128


def local(
    residual,
    context,
    out_proj,
    norm_gain,
    router_weight,
    block_modality,
    expert_rows,
    gate_weight,
    up_weight,
    down_weight,
):
    full_context = lax.all_gather(context, ("mod", "fsdp"), axis=1, tiled=True)
    token_count = residual.shape[0]
    projected = jnp.dot(
        full_context,
        lax.all_gather(out_proj, "tok", axis=0, tiled=True),
        preferred_element_type=jnp.float32,
    )
    hidden = residual.astype(jnp.float32) + projected
    token_mod = jnp.repeat(block_modality, BLOCK)
    gain_table = norm_gain.astype(jnp.float32)
    token_gain = jnp.where(token_mod[:, None] == 0, gain_table[0][None, :], gain_table[1][None, :])
    gained = hidden * token_gain
    router_table = router_weight.astype(jnp.float32)
    squares = jnp.sum(hidden * hidden, axis=1)
    square_total = lax.psum(squares, ("mod", "fsdp"))
    inverse = lax.rsqrt(square_total / D + 1e-05)
    normed = gained * inverse[:, None]
    logits = lax.psum(
        jnp.dot(normed, router_table, precision=lax.Precision.HIGHEST), ("mod", "fsdp")
    )
    score = jax.nn.sigmoid(logits)
    normed_rows = normed.astype(jnp.bfloat16)
    local_experts = gate_weight.shape[0]
    first_expert = lax.axis_index("mod") * local_experts
    row_ids = lax.iota(jnp.int32, token_count)
    own_rows = lax.dynamic_slice_in_dim(expert_rows, first_expert, local_experts, 0)
    own_pick = (own_rows[:, :, None] == row_ids[None, None, :]).astype(jnp.bfloat16)
    half_rows = lax.all_gather(normed_rows, "mod", axis=1, tiled=True)
    chosen = jnp.einsum(
        "ecr,rd->ecd", own_pick, half_rows, preferred_element_type=jnp.float32
    ).astype(jnp.bfloat16)
    unit_count = gate_weight.shape[2]
    piece = lax.all_gather(chosen, "tok", axis=1, tiled=True)
    gate_part = jnp.einsum("esd,edf->esf", piece, gate_weight, preferred_element_type=jnp.float32)
    up_part = jnp.einsum("esd,edf->esf", piece, up_weight, preferred_element_type=jnp.float32)
    partial_in = jnp.concatenate((gate_part, up_part), axis=2)
    summed_in = lax.psum(partial_in.astype(jnp.bfloat16), "fsdp").astype(jnp.float32)
    activation = (jax.nn.silu(summed_in[:, :, :unit_count]) * summed_in[:, :, unit_count:]).astype(
        jnp.bfloat16
    )
    expert_value = lax.psum_scatter(
        jnp.einsum(
            "esf,efd->sed", activation, down_weight, preferred_element_type=jnp.float32
        ).astype(jnp.bfloat16),
        "tok",
        scatter_dimension=0,
        tiled=True,
    ).astype(jnp.float32)
    own_score = lax.dynamic_slice_in_dim(score, first_expert, local_experts, 1)
    pick_table = own_pick.astype(jnp.float32)
    slot_score = jnp.einsum("ecr,re->ce", pick_table, own_score, precision=lax.Precision.HIGHEST)
    scaled = expert_value * slot_score[:, :, None]
    mixed_rows = jnp.einsum("ecr,ced->rd", pick_table, scaled, precision=lax.Precision.HIGHEST)
    combined = lax.psum_scatter(
        mixed_rows.astype(jnp.bfloat16), "mod", scatter_dimension=1, tiled=True
    )
    return combined


def solution(mesh):
    placed = (
        P(("groups", "tok"), ("fsdp", "mod")),
        P(("groups", "tok"), ("mod", "fsdp")),
        P("tok", ("fsdp", "mod")),
        P(None, ("fsdp", "mod")),
        P(("fsdp", "mod"), None),
        P(("groups", "tok")),
        P(None, ("groups", "tok")),
        P("mod", "fsdp", "tok"),
        P("mod", "fsdp", "tok"),
        P("mod", "tok", "fsdp"),
    )
    return jax.shard_map(
        local,
        mesh=mesh,
        in_specs=placed,
        out_specs=P(("groups", "tok"), ("fsdp", "mod")),
        check_vma=False,
    )
```

profile of v0, /device:TPU:0, one launch (start us, length us, event | category | flops | bytes accessed | tf_op | source)
XLA Modules:
  0.0 316.3 jit_solution(1377281258367514044)
XLA Ops:
  6.5 0.0 copy-start
  6.5 0.0 all-gather.3.cloned.1.call-start
  6.5 0.7 all-gather.3.cloned.1.call-update
  7.3 0.0 all-gather.5.cloned.1.call-start
  7.3 0.7 all-gather.5.cloned.1.call-update
  8.0 0.0 all-reduce.2.cloned.1.call-start
  8.7 0.7 convert_element_type.35
  9.4 0.7 constant_dynamic-slice_fusion.1
  10.1 18.3 %all-gather.3.cloned.1.call-done = bf16[128,4096]{1,0:T(8,128)(2,1)} async-done(((bf16[128,1024]{1,0:T(8,128)(2,1)}), bf16[128,4096]{1,0:T(8,128)(2,1)}) %all-gather.3.cloned.1.call-update) | async-done | bytes 1048592 | tf_op jit(solution)/shard_map/all_gather | solution.py:22
  28.4 151.2 %all-gather.5.cloned.1.call-done = bf16[4096,1024]{1,0:T(8,128)(2,1)} async-done(((bf16[1024,1024]{1,0:T(8,128)(2,1)}), bf16[4096,1024]{1,0:T(8,128)(2,1)}) %all-gather.5.cloned.1.call-update) | async-done | bytes 8388624 | tf_op jit(solution)/shard_map/all_gather | solution.py:26
  179.6 5.0 %multiply_reduce_fusion = (f32[128]{0:T(128)S(1)}, f32[128,1024]{1,0:T(8,128)S(1)}) fusion(bf16[128,4096]{1,0:T(8,128)(2,1)} %all-gather.3.cloned.1.call-done, bf16[4096,1024]{1,0:T(8,128)(2,1)} %all-gather.5.cloned.1.call-done, bf16[128,1024]{1,0:T(8,128)(2,1)} %param.10), kind=kOutput, calls=%fused_computation.13 | convolution fusion | flops 1074265984 | bytes 10224128 | tf_op jit(solution)/shard_map/dot_general | solution.py:24
  184.6 6.8 %psum.21 = f32[128]{0:T(128)S(1)} all-reduce(f32[128]{0:T(128)S(1)} %get-tuple-element.5), channel_id=1, replica_groups=mesh['groups'=2,'tok'=4,'mod'=2,'fsdp'=2] {'mod','fsdp'}, use_global_device_ids=true, to_apply=%region_1.2 | all-reduce | flops 128 | bytes 1024 | tf_op jit(solution)/shard_map/psum | solution.py:36
  191.5 0.1 fusion.7
  191.6 7.6 %all_gather.14 = bf16[128,2048]{1,0:T(8,128)(2,1)S(1)} all-gather(bf16[128,1024]{1,0:T(8,128)(2,1)S(1)} %fusion.7), channel_id=1, replica_groups=mesh['groups'=2,'tok'=4,'mod'=2,'fsdp'=2] {'mod'}, dimensions={1}, use_global_device_ids=true | all-gather | bytes 786432 | tf_op jit(solution)/shard_map/all_gather | solution.py:49
  199.1 0.2 convolution_convert_fusion.3
  199.4 14.7 %all_gather.15 = bf16[2,64,2048]{2,1,0:T(8,128)(2,1)S(1)} all-gather(bf16[2,16,2048]{2,1,0:T(8,128)(2,1)S(1)} %convolution_convert_fusion.3), channel_id=1, replica_groups=mesh['groups'=2,'tok'=4,'mod'=2,'fsdp'=2] {'tok'}, dimensions={1}, use_global_device_ids=true | all-gather | bytes 655360 | tf_op jit(solution)/shard_map/all_gather | solution.py:54
  214.1 11.3 %convolution_convert_fusion = bf16[2,64,2752]{2,1,0:T(8,128)(2,1)S(1)} fusion(bf16[2,64,2048]{2,1,0:T(8,128)(2,1)S(1)} %all_gather.15, bf16[2,2048,2752]{1,2,0:T(8,128)(2,1)} %param.18), kind=kOutput, calls=%fused_computation | convolution fusion | flops 1443192832 | bytes 23773184 | tf_op jit(solution)/shard_map/esd,edf->esf/dot_general | solution.py:56
  225.4 11.3 %convolution_convert_fusion.1 = bf16[2,64,2752]{2,1,0:T(8,128)(2,1)S(1)} fusion(bf16[2,64,2048]{2,1,0:T(8,128)(2,1)S(1)} %all_gather.15, bf16[2,2048,2752]{1,2,0:T(8,128)(2,1)} %param.17), kind=kOutput, calls=%fused_computation.1 | convolution fusion | flops 1443192832 | bytes 23773184 | tf_op jit(solution)/shard_map/esd,edf->esf/dot_general | solution.py:55
  236.7 1.4 pad_maximum_fusion
  238.1 0.0 all-reduce.2.cloned.1.call-update
  238.1 0.0 reduce-scatter.3.cloned.1.call-start
  238.2 19.4 %all-reduce.2.cloned.1.call-done = bf16[2,64,5504]{2,1,0:T(8,128)(2,1)} async-done(((bf16[2,64,5504]{2,1,0:T(8,128)(2,1)}), bf16[2,64,5504]{2,1,0:T(8,128)(2,1)}) %all-reduce.2.cloned.1.call-update) | async-done | bytes 1409040 | tf_op jit(solution)/shard_map/psum | solution.py:58
  257.6 1.5 convert_element_type.38
  259.1 12.3 %fusion.1 = bf16[64,2,2048]{2,0,1:T(8,128)(2,1)} fusion(bf16[2,2752,2048]{2,1,0:T(8,128)(2,1)} %param.19, f32[2,64,5504]{2,1,0:T(8,128)S(1)} %convert_element_type.38), kind=kOutput, calls=%fused_computation.5 | convolution fusion | flops 1445216256 | bytes 25952256 | tf_op jit(solution)/shard_map/esf,efd->sed/dot_general | solution.py:63
  271.4 0.0 reduce-scatter.3.cloned.1.call-update
  271.4 0.0 reduce-scatter.5.cloned.1.call-start
  271.5 0.0 copy-done
  271.5 0.4 fusion.6
  271.9 7.3 %psum.23 = f32[128,4]{0,1:T(4,128)S(1)} all-reduce(f32[128,4]{0,1:T(4,128)S(1)} %fusion.6), channel_id=1, replica_groups=mesh['groups'=2,'tok'=4,'mod'=2,'fsdp'=2] {'mod','fsdp'}, use_global_device_ids=true, to_apply=%region_4.5 | all-reduce | flops 512 | bytes 4096 | tf_op jit(solution)/shard_map/psum | solution.py:39
  279.2 0.2 fusion.13
  279.4 15.0 %reduce-scatter.3.cloned.1.call-done = bf16[16,2,2048]{2,0,1:T(8,128)(2,1)} async-done(((bf16[64,2,2048]{2,0,1:T(8,128)(2,1)}), bf16[16,2,2048]{2,0,1:T(8,128)(2,1)}) %reduce-scatter.3.cloned.1.call-update) | async-done | bytes 131088 | tf_op jit(solution)/shard_map/reduce_scatter | solution.py:62
  294.4 2.4 fusion
  296.8 0.0 reduce-scatter.5.cloned.1.call-update
  296.8 12.9 %reduce-scatter.5.cloned.1.call-done = bf16[128,1024]{1,0:T(8,128)(2,1)} async-done(((bf16[128,2048]{1,0:T(8,128)(2,1)}), bf16[128,1024]{1,0:T(8,128)(2,1)}) %reduce-scatter.5.cloned.1.call-update) | async-done | bytes 262160 | tf_op jit(solution)/shard_map/reduce_scatter | solution.py:75
  (4 shorter events, 0.0 us)
Async XLA Ops:
  6.5 264.9 %copy-start = (bf16[1024,4]{0,1:T(4,128)(2,1)S(1)}, bf16[1024,4]{0,1:T(4,128)(2,1)}, u32[]{:S(2)}) copy-start(bf16[1024,4]{0,1:T(4,128)(2,1)} %param.14) | copy-start | bytes 24580
  6.5 21.8 %all-gather.3.cloned.1.call-start = ((), (), s32[]{:S(2)}) async-start(), calls=%async_computation.2 | async-start | bytes 1310720 | tf_op jit(solution)/shard_map/all_gather | solution.py:22
  7.3 172.4 %all-gather.5.cloned.1.call-start = ((), (), s32[]{:S(2)}) async-start(), calls=%async_computation.3 | async-start | bytes 10485760 | tf_op jit(solution)/shard_map/all_gather | solution.py:26
  8.0 249.5 %all-reduce.2.cloned.1.call-start = ((), (), s32[]{:S(2)}) async-start(), calls=%async_computation.4 | async-start | bytes 2818048 | tf_op jit(solution)/shard_map/psum | solution.py:58
  238.1 56.3 %reduce-scatter.3.cloned.1.call-start = ((), (), s32[]{:S(2)}) async-start(), calls=%async_computation.5 | async-start | bytes 655360 | tf_op jit(solution)/shard_map/reduce_scatter | solution.py:62
  271.4 38.4 %reduce-scatter.5.cloned.1.call-start = ((), (), s32[]{:S(2)}) async-start(), calls=%async_computation.6 | async-start | bytes 786432 | tf_op jit(solution)/shard_map/reduce_scatter | solution.py:75
Sparse Core Ops, SparseCore 0:
  8.9 19.4 all-gather.2
  29.9 149.6 all-gather.4
  238.2 19.2 all-reduce.1
  271.5 22.8 reduce-scatter.2
  296.9 12.7 reduce-scatter.4
where the time goes:
time: 317 us; the launch traced here: 316 us
  waiting for transfers between devices  218 us (69%)
  matrix products  43.1 us (14%)
  blocking collectives  36.4 us (11%)
  between operations  13.8 us (4%)
  other arithmetic  3.74 us (1%)
    all_gather x1, waiting for transfers between devices, local(): lax.all_gather(out_proj, 'tok', axis=0, tiled=True)  151 us
    psum x1, waiting for transfers between devices, local(): lax.psum(partial_in.astype(jnp.bfloat16), 'fsdp').astype(jnp.float32)  19.4 us
    all_gather x1, waiting for transfers between devices, local(): full_context = lax.all_gather(context, ('mod', 'fsdp'), axis=1, tiled=True)  18.3 us
    reduce_scatter x1, waiting for transfers between devices, local(): lax.psum_scatter(jnp.einsum('esf,efd->sed', activation, down_weight, pref...  15 us
    all_gather x1, blocking collectives, local(): piece = lax.all_gather(chosen, 'tok', axis=1, tiled=True)  14.7 us
    reduce_scatter x1, waiting for transfers between devices, local(): lax.psum_scatter(mixed_rows.astype(jnp.bfloat16), 'mod', scatter_dimensio...  12.9 us
    dot_general x1, matrix products, local(): jnp.einsum('esf,efd->sed', activation, down_weight, preferred_element_typ...  12.3 us
    dot_general x1, matrix products, local(): jnp.einsum('esd,edf->esf', piece, gate_weight, preferred_element_type=jnp...  11.3 us
  transfers between devices with their start and end apart: 5, of which 5 were waited for; matrix products, arithmetic and copies ran while one was open for 1% of the time, Pallas kernels for 0%

commit v1 on v0

--- a/solution.py
+++ b/solution.py
@@ -5,6 +5,28 @@
 
 D = 4096
 BLOCK = 128
+
+
+def joined_along(blocks, dim):
+    blocks = jnp.moveaxis(blocks, 0, dim)
+    shape = blocks.shape
+    return blocks.reshape(*shape[:dim], shape[dim] * shape[dim + 1], *shape[dim + 2 :])
+
+
+def ring_gather(x, axis, dim):
+    devices = lax.axis_size(axis)
+    pairs = [(i, (i + 1) % devices) for i in range(devices)]
+    back = [(b, a) for a, b in pairs]
+    lower, upper = ([], [])
+    for step in range(devices - 1):
+        if step % 2 == 0:
+            lower.append(lax.ppermute(lower[-1] if lower else x, axis, pairs))
+        else:
+            upper.append(lax.ppermute(upper[-1] if upper else x, axis, back))
+    blocks = jnp.stack([*lower[::-1], x, *upper])
+    shift = lax.axis_index(axis) - len(lower)
+    blocks = blocks[(jnp.arange(devices) - shift) % devices]
+    return joined_along(blocks, dim)
 
 
 def local(
@@ -51,7 +73,7 @@
         "ecr,rd->ecd", own_pick, half_rows, preferred_element_type=jnp.float32
     ).astype(jnp.bfloat16)
     unit_count = gate_weight.shape[2]
-    piece = lax.all_gather(chosen, "tok", axis=1, tiled=True)
+    piece = ring_gather(chosen, "tok", 1)
     gate_part = jnp.einsum("esd,edf->esf", piece, gate_weight, preferred_element_type=jnp.float32)
     up_part = jnp.einsum("esd,edf->esf", piece, up_weight, preferred_element_type=jnp.float32)
     partial_in = jnp.concatenate((gate_part, up_part), axis=2)

time: 317 us -> 316 us (level)
  blocking collectives: 36.4 us -> 21.7 us
  waiting for transfers between devices: 218 us -> 228 us
  starting transfers between devices: 0.16 us -> 4.03 us
    all_gather x1 -> x0, blocking collectives: 14.7 us -> none  [local(): piece = lax.all_gather(chosen, 'tok', axis=1, tiled=True)]
    ppermute x0 -> x3, waiting for transfers between devices: none -> 9.77 us  [the longest x2 9.77 us: ring_gather(): lower.append(lax.ppermute(lower[-1] if lower else x, axis, pairs))]
    ppermute x0 -> x3, starting transfers between devices: none -> 3.87 us  [the longest x1 3.81 us: ring_gather(): upper.append(lax.ppermute(upper[-1] if upper else x, axis, back))]
  transfers between devices with their start and end apart: 5 -> 8, of which waited for: 5 -> 7; matrix products, arithmetic and copies ran while one was open for 1% -> 1% of each run, Pallas kernels for 0% -> 0%
where the time goes in v1:
time: 316 us; the launch traced here: 315 us
  waiting for transfers between devices  228 us (72%)
  matrix products  43.1 us (14%)
  blocking collectives  21.7 us (7%)
  between operations  13.9 us (4%)
  starting transfers between devices  4.03 us (1%)
  other arithmetic  3.81 us (1%)
    all_gather x1, waiting for transfers between devices, local(): lax.all_gather(out_proj, 'tok', axis=0, tiled=True)  151 us
    psum x1, waiting for transfers between devices, local(): lax.psum(partial_in.astype(jnp.bfloat16), 'fsdp').astype(jnp.float32)  18.9 us
    all_gather x1, waiting for transfers between devices, local(): full_context = lax.all_gather(context, ('mod', 'fsdp'), axis=1, tiled=True)  18.3 us
    reduce_scatter x1, waiting for transfers between devices, local(): lax.psum_scatter(jnp.einsum('esf,efd->sed', activation, down_weight, pref...  15 us
    reduce_scatter x1, waiting for transfers between devices, local(): lax.psum_scatter(mixed_rows.astype(jnp.bfloat16), 'mod', scatter_dimensio...  12.9 us
    dot_general x1, matrix products, local(): jnp.einsum('esf,efd->sed', activation, down_weight, preferred_element_typ...  12.3 us
    dot_general x1, matrix products, local(): jnp.einsum('esd,edf->esf', piece, gate_weight, preferred_element_type=jnp...  11.3 us
    dot_general x1, matrix products, local(): jnp.einsum('esd,edf->esf', piece, up_weight, preferred_element_type=jnp.f...  11.3 us
  transfers between devices with their start and end apart: 8, of which 7 were waited for; matrix products, arithmetic and copies ran while one was open for 1% of the time, Pallas kernels for 0%

profile of v1, /device:TPU:0, one launch (start us, length us, event | category | flops | bytes accessed | tf_op | source)
XLA Modules:
  0.0 315.4 jit_solution(17556617156485565791)
XLA Ops:
  6.5 0.0 copy-start
  6.5 0.0 all-gather.3.cloned.1.call-start
  6.5 0.7 all-gather.3.cloned.1.call-update
  7.3 0.0 all-gather.5.cloned.1.call-start
  7.3 0.7 all-gather.5.cloned.1.call-update
  8.0 0.0 all-reduce.2.cloned.1.call-start
  8.7 0.7 convert_element_type.35
  9.4 0.7 constant_dynamic-slice_fusion.1
  10.1 18.3 %all-gather.3.cloned.1.call-done = bf16[128,4096]{1,0:T(8,128)(2,1)} async-done(((bf16[128,1024]{1,0:T(8,128)(2,1)}), bf16[128,4096]{1,0:T(8,128)(2,1)}) %all-gather.3.cloned.1.call-update) | async-done | bytes 1048592 | tf_op jit(solution)/shard_map/all_gather | solution.py:44
  28.4 151.2 %all-gather.5.cloned.1.call-done = bf16[4096,1024]{1,0:T(8,128)(2,1)} async-done(((bf16[1024,1024]{1,0:T(8,128)(2,1)}), bf16[4096,1024]{1,0:T(8,128)(2,1)}) %all-gather.5.cloned.1.call-update) | async-done | bytes 8388624 | tf_op jit(solution)/shard_map/all_gather | solution.py:48
  179.6 5.0 %multiply_reduce_fusion = (f32[128]{0:T(128)S(1)}, f32[128,1024]{1,0:T(8,128)S(1)}) fusion(bf16[128,4096]{1,0:T(8,128)(2,1)} %all-gather.3.cloned.1.call-done, bf16[4096,1024]{1,0:T(8,128)(2,1)} %all-gather.5.cloned.1.call-done, bf16[128,1024]{1,0:T(8,128)(2,1)} %param.10), kind=kOutput, calls=%fused_computation.15 | convolution fusion | flops 1074265984 | bytes 10224128 | tf_op jit(solution)/shard_map/dot_general | solution.py:46
  184.6 6.8 %psum.21 = f32[128]{0:T(128)S(1)} all-reduce(f32[128]{0:T(128)S(1)} %get-tuple-element.5), channel_id=1, replica_groups=mesh['groups'=2,'tok'=4,'mod'=2,'fsdp'=2] {'mod','fsdp'}, use_global_device_ids=true, to_apply=%region_1.2 | all-reduce | flops 128 | bytes 1024 | tf_op jit(solution)/shard_map/psum | solution.py:58
  191.5 0.1 fusion.7
  191.6 7.6 %all_gather.11 = bf16[128,2048]{1,0:T(8,128)(2,1)S(1)} all-gather(bf16[128,1024]{1,0:T(8,128)(2,1)S(1)} %fusion.7), channel_id=1, replica_groups=mesh['groups'=2,'tok'=4,'mod'=2,'fsdp'=2] {'mod'}, dimensions={1}, use_global_device_ids=true | all-gather | bytes 786432 | tf_op jit(solution)/shard_map/all_gather | solution.py:71
  199.1 0.2 convolution_convert_fusion.3
  199.4 0.1 collective-permute-start
  199.5 3.8 %collective-permute-start.2 = (bf16[2,16,2048]{2,1,0:T(8,128)(2,1)S(1)}, bf16[2,16,2048]{2,1,0:T(8,128)(2,1)S(1)}, u32[]{:S(2)}, u32[]{:S(2)}) collective-permute-start(bf16[2,16,2048]{2,1,0:T(8,128)(2,1)S(1)} %convolution_convert_fusion.3), channel_id=1, source_target_pairs={{4,0},{8,4},{12,8},{0,12},{5,1},{9,5},{13,9},{1,13},{6,2},{10,6},{... | collective-permute-start | bytes 393224 | tf_op jit(solution)/shard_map/ppermute | solution.py:25
  203.3 3.0 collective-permute-done
  206.3 0.0 collective-permute-start.1
  206.3 0.0 collective-permute-done.2
  206.4 6.7 %collective-permute-done.1 = bf16[2,16,2048]{2,1,0:T(8,128)(2,1)S(1)} collective-permute-done((bf16[2,16,2048]{2,1,0:T(8,128)(2,1)S(1)}, bf16[2,16,2048]{2,1,0:T(8,128)(2,1)S(1)}, u32[]{:S(2)}, u32[]{:S(2)}) %collective-permute-start.1) | collective-permute-done | bytes 131104 | tf_op jit(solution)/shard_map/ppermute | solution.py:23
  213.1 0.1 pad_maximum_fusion.1
  213.1 0.6 gather_fusion
  213.8 11.3 %convolution_convert_fusion = bf16[2,64,2752]{2,1,0:T(8,128)(2,1)S(1)} fusion(bf16[2,64,2048]{2,1,0:T(8,128)(2,1)S(1)} %bitcast.35, bf16[2,2048,2752]{1,2,0:T(8,128)(2,1)} %param.18), kind=kOutput, calls=%fused_computation.1 | convolution fusion | flops 1443192832 | bytes 23773184 | tf_op jit(solution)/shard_map/esd,edf->esf/dot_general | solution.py:78
  225.1 11.3 %convolution_convert_fusion.1 = bf16[2,64,2752]{2,1,0:T(8,128)(2,1)S(1)} fusion(bf16[2,64,2048]{2,1,0:T(8,128)(2,1)S(1)} %bitcast.36, bf16[2,2048,2752]{1,2,0:T(8,128)(2,1)} %param.17), kind=kOutput, calls=%fused_computation.2 | convolution fusion | flops 1443192832 | bytes 23773184 | tf_op jit(solution)/shard_map/esd,edf->esf/dot_general | solution.py:77
  236.4 1.4 pad_maximum_fusion
  237.8 0.0 all-reduce.2.cloned.1.call-update
  237.8 0.0 reduce-scatter.3.cloned.1.call-start
  237.8 18.9 %all-reduce.2.cloned.1.call-done = bf16[2,64,5504]{2,1,0:T(8,128)(2,1)} async-done(((bf16[2,64,5504]{2,1,0:T(8,128)(2,1)}), bf16[2,64,5504]{2,1,0:T(8,128)(2,1)}) %all-reduce.2.cloned.1.call-update) | async-done | bytes 1409040 | tf_op jit(solution)/shard_map/psum | solution.py:80
  256.7 1.5 convert_element_type.38
  258.2 12.3 %fusion.1 = bf16[64,2,2048]{2,0,1:T(8,128)(2,1)} fusion(bf16[2,2752,2048]{2,1,0:T(8,128)(2,1)} %param.19, f32[2,64,5504]{2,1,0:T(8,128)S(1)} %convert_element_type.38), kind=kOutput, calls=%fused_computation.6 | convolution fusion | flops 1445216256 | bytes 25952256 | tf_op jit(solution)/shard_map/esf,efd->sed/dot_general | solution.py:85
  270.5 0.0 reduce-scatter.3.cloned.1.call-update
  270.6 0.0 reduce-scatter.5.cloned.1.call-start
  270.6 0.0 copy-done
  270.6 0.4 fusion.6
  271.0 7.3 %psum.23 = f32[128,4]{0,1:T(4,128)S(1)} all-reduce(f32[128,4]{0,1:T(4,128)S(1)} %fusion.6), channel_id=1, replica_groups=mesh['groups'=2,'tok'=4,'mod'=2,'fsdp'=2] {'mod','fsdp'}, use_global_device_ids=true, to_apply=%region_4.5 | all-reduce | flops 512 | bytes 4096 | tf_op jit(solution)/shard_map/psum | solution.py:61
  278.3 0.2 fusion.13
  278.5 15.0 %reduce-scatter.3.cloned.1.call-done = bf16[16,2,2048]{2,0,1:T(8,128)(2,1)} async-done(((bf16[64,2,2048]{2,0,1:T(8,128)(2,1)}), bf16[16,2,2048]{2,0,1:T(8,128)(2,1)}) %reduce-scatter.3.cloned.1.call-update) | async-done | bytes 131088 | tf_op jit(solution)/shard_map/reduce_scatter | solution.py:84
  293.5 2.4 fusion
  295.9 0.0 reduce-scatter.5.cloned.1.call-update
  296.0 12.9 %reduce-scatter.5.cloned.1.call-done = bf16[128,1024]{1,0:T(8,128)(2,1)} async-done(((bf16[128,2048]{1,0:T(8,128)(2,1)}), bf16[128,1024]{1,0:T(8,128)(2,1)}) %reduce-scatter.5.cloned.1.call-update) | async-done | bytes 262160 | tf_op jit(solution)/shard_map/reduce_scatter | solution.py:97
  (7 shorter events, 0.1 us)
Async XLA Ops:
  6.5 264.1 %copy-start = (bf16[1024,4]{0,1:T(4,128)(2,1)S(1)}, bf16[1024,4]{0,1:T(4,128)(2,1)}, u32[]{:S(2)}) copy-start(bf16[1024,4]{0,1:T(4,128)(2,1)} %param.14) | copy-start | bytes 24580
  6.5 21.8 %all-gather.3.cloned.1.call-start = ((), (), s32[]{:S(2)}) async-start(), calls=%async_computation.2 | async-start | bytes 1310720 | tf_op jit(solution)/shard_map/all_gather | solution.py:44
  7.3 172.4 %all-gather.5.cloned.1.call-start = ((), (), s32[]{:S(2)}) async-start(), calls=%async_computation.3 | async-start | bytes 10485760 | tf_op jit(solution)/shard_map/all_gather | solution.py:48
  8.0 248.7 %all-reduce.2.cloned.1.call-start = ((), (), s32[]{:S(2)}) async-start(), calls=%async_computation.4 | async-start | bytes 2818048 | tf_op jit(solution)/shard_map/psum | solution.py:80
  199.4 6.9 %collective-permute-start = (bf16[2,16,2048]{2,1,0:T(8,128)(2,1)S(1)}, bf16[2,16,2048]{2,1,0:T(8,128)(2,1)S(1)}, u32[]{:S(2)}, u32[]{:S(2)}) collective-permute-start(bf16[2,16,2048]{2,1,0:T(8,128)(2,1)S(1)} %convolution_convert_fusion.3), channel_id=1, source_target_pairs={{0,4},{4,8},{8,12},{12,0},{1,5},{5,9},{9,13},{13,1},{2,6},{6,10},{... | collective-permute-start | bytes 393224 | tf_op jit(solution)/shard_map/ppermute | solution.py:23
  199.5 6.9 %collective-permute-start.2 = (bf16[2,16,2048]{2,1,0:T(8,128)(2,1)S(1)}, bf16[2,16,2048]{2,1,0:T(8,128)(2,1)S(1)}, u32[]{:S(2)}, u32[]{:S(2)}) collective-permute-start(bf16[2,16,2048]{2,1,0:T(8,128)(2,1)S(1)} %convolution_convert_fusion.3), channel_id=1, source_target_pairs={{4,0},{8,4},{12,8},{0,12},{5,1},{9,5},{13,9},{1,13},{6,2},{10,6},{... | collective-permute-start | bytes 393224 | tf_op jit(solution)/shard_map/ppermute | solution.py:25
  206.3 6.8 %collective-permute-start.1 = (bf16[2,16,2048]{2,1,0:T(8,128)(2,1)S(1)}, bf16[2,16,2048]{2,1,0:T(8,128)(2,1)S(1)}, u32[]{:S(2)}, u32[]{:S(2)}) collective-permute-start(bf16[2,16,2048]{2,1,0:T(8,128)(2,1)S(1)} %collective-permute-done), channel_id=1, source_target_pairs={{0,4},{4,8},{8,12},{12,0},{1,5},{5,9},{9,13},{13,1},{2,6},{6,10},{... | collective-permute-start | bytes 393224 | tf_op jit(solution)/shard_map/ppermute | solution.py:23
  237.8 55.7 %reduce-scatter.3.cloned.1.call-start = ((), (), s32[]{:S(2)}) async-start(), calls=%async_computation.5 | async-start | bytes 655360 | tf_op jit(solution)/shard_map/reduce_scatter | solution.py:84
  270.6 38.3 %reduce-scatter.5.cloned.1.call-start = ((), (), s32[]{:S(2)}) async-start(), calls=%async_computation.6 | async-start | bytes 786432 | tf_op jit(solution)/shard_map/reduce_scatter | solution.py:97
Sparse Core Ops, SparseCore 0:
  8.9 19.4 all-gather.2
  29.9 149.6 all-gather.4
  237.9 18.7 all-reduce.1
  270.7 22.8 reduce-scatter.2
  296.1 12.7 reduce-scatter.4
